TPU v7x, 32 devices: a whole 2x2x4 slice. The times are simulated.
32 devices in a mesh: leaf: 2 (over x), rows: 16 (over z, y, core).
Axes of the slice: x: 2, y: 2, z: 4, core: 2. Of those that a mesh axis runs over, the one named last changes fastest.
Arguments:
- features: bfloat16 [262144, 256], P(('leaf', 'rows')), parts along dimension 0, may hold values from -80 to 80
- node_ids: int32 [262144], P(('leaf', 'rows')), parts along dimension 0, may hold values from -1 to 15, as said below
- labels: int32 [262144], P(('leaf', 'rows')), parts along dimension 0, may hold values from 0 to 15
- owners: int32 [32], P('leaf'), parts along dimension 0, may hold values from 0 to 15, each once
Outputs:
- hyperplanes: float32 [32, 16, 256], P(('leaf', 'rows')), parts along dimension 0
- scores: float32 [16, 262144], P(None, ('leaf', 'rows')), parts along dimension 1
There are 2 independent parts, one for each index of `leaf`. A program takes and returns all parts, laid end to end along the dimension named above; each array names one. Nothing has to cross between parts.
Inputs may be any that keep to these rules, and one draw needn't show every extreme that they name: `node_ids`: on rows device d, row p of node n's segment (local row n * 512 + p) holds n or -1; the live rows of a segment come first and there is at least one; some segment of every device is full. Each node number appears once in owners; node n is owned by the device of rows with index owners[n].
All inputs are finite; a program needn't handle non-finite values.
Results may differ from a plain program's by a relative error of at most 0.0035.
Values may be sent and summed in bfloat16 or wider, within the bound.
A program may use at most 128 MiB of HBM per device.

v0:
```python
import jax
import jax.numpy as jnp
from jax import lax
from jax.sharding import PartitionSpec as P

CLASSES = 16


ridge_term = 0.1


def solve_nodes(scatter, sums, counts):
    totals = jnp.sum(counts, axis=1)
    centers = jnp.sum(sums, axis=1) / totals[:, None]
    scaled = sums / jnp.maximum(counts, 1.0)[:, :, None]
    within = scatter - jnp.einsum("ncf,ncg->nfg", scaled, sums, precision=lax.Precision.HIGHEST)
    identity = jnp.eye(scatter.shape[-1], dtype=jnp.float32)
    system = within / totals[:, None, None] + ridge_term * identity
    shifts = (sums - counts[:, :, None] * centers[:, None, :]) / totals[:, None, None]
    factor = jnp.linalg.cholesky(system)
    planes = jax.vmap(lambda lower, right: jax.scipy.linalg.cho_solve((lower, True), right.T).T)(
        factor, shifts
    )
    offsets = -jnp.einsum("ncf,nf->nc", planes, centers, precision=lax.Precision.HIGHEST)
    return (planes, offsets)


def on_device(features, node_ids, labels, owners):
    row_count, feature_count = features.shape
    node_count = owners.shape[0]
    segment = row_count // node_count
    inverse = (
        jnp.zeros((node_count,), jnp.int32).at[owners].set(jnp.arange(node_count, dtype=jnp.int32))
    )
    blocks = jnp.take(features.reshape(node_count, segment, feature_count), inverse, axis=0)
    slot_ids = jnp.take(node_ids.reshape(node_count, segment), inverse, axis=0)
    marks = jnp.take(labels.reshape(node_count, segment), inverse, axis=0)
    live_rows = slot_ids == inverse[:, None]
    masked = jnp.where(live_rows[:, :, None], blocks, jnp.zeros((), jnp.bfloat16))
    classes = jnp.arange(CLASSES, dtype=jnp.int32)
    tagged = jnp.where(live_rows, marks, -1).astype(jnp.bfloat16)
    arrived, arrived_tags = (
        lax.all_to_all(masked, "rows", split_axis=0, concat_axis=1, tiled=True),
        lax.all_to_all(tagged, "rows", split_axis=0, concat_axis=1, tiled=True),
    )
    owner_tags = arrived_tags.astype(jnp.int32)
    owner_hot = (owner_tags[:, None, :] == classes[None, :, None]).astype(jnp.bfloat16)
    mine_sums = jnp.einsum("ncs,nsf->ncf", owner_hot, arrived, preferred_element_type=jnp.float32)
    mine_counts = jnp.sum(owner_hot.astype(jnp.float32), axis=2)
    scatter = jnp.einsum("nsf,nsg->nfg", arrived, arrived, preferred_element_type=jnp.float32)
    planes, offsets = solve_nodes(scatter, mine_sums, mine_counts)
    every_planes, every_offsets = (
        lax.all_gather(planes, "rows", axis=0, tiled=True),
        lax.all_gather(offsets, "rows", axis=0, tiled=True),
    )
    rounded = every_planes.astype(jnp.bfloat16)
    result = jnp.einsum("ncf,nsf->cns", rounded, blocks, preferred_element_type=jnp.float32)
    result = result + every_offsets.T[:, :, None]
    result = jnp.where(live_rows[None], result, 0.0)
    result = jnp.take(result, owners, axis=1).reshape(CLASSES, row_count)
    return (planes, result)


def solution(mesh):
    in_specs = (P(("leaf", "rows"), None), P(("leaf", "rows")), P(("leaf", "rows")), P("leaf"))
    out_specs = (P(("leaf", "rows"), None, None), P(None, ("leaf", "rows")))
    return jax.shard_map(
        on_device, mesh=mesh, in_specs=in_specs, out_specs=out_specs, check_vma=False
    )
```

profile of v0, /device:TPU:0, one launch (start us, length us, event | category | flops | bytes accessed | tf_op | source)
XLA Modules:
  0.0 252.2 jit_solution(4196847479306877663)
XLA Ops:
  1.9 0.7 compare_and_fusion
  2.6 0.8 reshape.307
  3.4 0.8 reshape.309
  7.2 7.4 %all-to-all-start.1 = ((bf16[16,2,256]{2,1,0:T(2,128)(2,1)}), bf16[16,2,256]{2,1,0:T(2,128)(2,1)S(1)}, u32[]{:S(2)}, u32[]{:S(2)}) async-start(bf16[16,2,256]{2,1,0:T(2,128)(2,1)} %reshape.402), calls=%async_computation.1 | async-start | bytes 32768 | tf_op jit(solution)/shard_map/all_to_all | solution.py:44
  14.6 4.9 %gather_fusion = bf16[16,512,256]{2,1,0:T(8,128)(2,1)} fusion(bf16[16,512,256]{2,1,0:T(8,128)(2,1)} %bitcast.110, s32[1024]{0:T(1024)S(1)} %pad_clamp_fusion.1), kind=kCustom, calls=%fused_computation.2 | custom fusion | bytes 8388672 | tf_op jit(solution)/shard_map/jit(_take)/gather | solution.py:35
  19.5 5.3 %broadcast_select_fusion.1 = bf16[16,512,256]{2,1,0:T(8,128)(2,1)} fusion(pred[16,512]{1,0:T(8,128)(4,1)S(1)} %get-tuple-element.24, bf16[16,512,256]{2,1,0:T(8,128)(2,1)} %gather_fusion, pred[16]{0:T(512)(128)(4,1)S(1)} %get-tuple-element.35), kind=kLoop, calls=%fused_computation.8 | loop fusion | flops 4194304 | bytes 8396816 | tf_op jit(solution)/shard_map/jit(_where)/select_n | solution.py:39
  24.8 6.2 %all-to-all-start = ((bf16[16,512,256]{2,1,0:T(8,128)(2,1)}), bf16[16,512,256]{2,1,0:T(8,128)(2,1)}, u32[]{:S(2)}, u32[]{:S(2)}) async-start(bf16[16,512,256]{2,1,0:T(8,128)(2,1)} %broadcast_select_fusion.1), calls=%async_computation | async-start | bytes 8388608 | tf_op jit(solution)/shard_map/all_to_all | solution.py:43
  32.5 0.8 convert_reduce_fusion.1
  33.2 75.3 %all-to-all-done = bf16[16,512,256]{2,1,0:T(8,128)(2,1)} async-done(((bf16[16,512,256]{2,1,0:T(8,128)(2,1)}), bf16[16,512,256]{2,1,0:T(8,128)(2,1)}, u32[]{:S(2)}, u32[]{:S(2)}) %all-to-all-start) | async-done | bytes 4194336 | tf_op jit(solution)/shard_map/all_to_all | solution.py:43
  108.5 2.9 %fusion.33 = (f32[256]{0:T(256)S(1)}, f32[16,256]{1,0:T(8,128)S(1)}) fusion(bf16[8192,256]{1,0:T(8,128)(2,1)} %bitcast.4, s32[8192]{0:T(1024)S(1)} %bitcast.115), kind=kOutput, calls=%fused_computation.85 | convolution fusion | flops 67243776 | bytes 4244480 | tf_op jit(solution)/shard_map/ncs,nsf->ncf/dot_general | solution.py:48
  112.1 0.7 divide_bitcast_fusion
  112.8 5.2 %convolution_bitcast_fusion = f32[256,256]{0,1:T(8,128)S(1)} fusion(bf16[16,512,256]{2,1,0:T(8,128)(2,1)} %all-to-all-done), kind=kOutput, calls=%fused_computation.16 | convolution fusion | flops 1073741824 | bytes 4456448 | tf_op jit(solution)/shard_map/nsf,nsg->nfg/dot_general | solution.py:50
  118.0 1.1 fusion.5
  119.3 11.7 %custom-call.20 = f32[1,128,128]{2,1,0:T(8,128)S(1)} custom-call(f32[1,128,128]{2,1,0:T(8,128)S(1)} %cholesky.117), custom_call_target="Cholesky" | custom-call | tf_op jit(solution)/shard_map/jit(cholesky)/cholesky | solution.py:20
  131.0 9.8 %custom-call.21 = f32[1,1,128,128]{2,3,1,0:T(8,128)S(1)} custom-call(f32[1,1,128,128]{3,2,1,0:T(8,128)S(1)} %get-tuple-element.30), custom_call_target="InvertDiagBlocksLowerTriangular" | custom-call | tf_op jit(solution)/shard_map/jit(cholesky)/cholesky | solution.py:20
  141.3 11.9 %custom-call.22 = f32[1,128,128]{2,1,0:T(8,128)S(1)} custom-call(f32[1,128,128]{2,1,0:T(8,128)S(1)} %fusion.6), custom_call_target="Cholesky" | custom-call | tf_op jit(solution)/shard_map/jit(cholesky)/cholesky | solution.py:20
  155.9 3.9 %while.1 = (s32[]{:T(128)}, f32[1,256,256]{2,1,0:T(8,128)S(1)}, s32[2,2]{1,0:T(2,128)S(1)}, f32[2,1,128,128]{3,2,1,0:T(8,128)S(1)}, s32[]{:T(128)}) while((s32[]{:T(128)}, f32[1,256,256]{2,1,0:T(8,128)S(1)}, s32[2,2]{1,0:T(2,128)S(1)}, f32[2,1,128,128]{3,2,1,0:T(8,128)S(1)}, s32[]{:T(128)}) %tuple.32), condition=%wide.while_cond, body=%wide.while_body.sunk | while | flops 2 | bytes 131181 | solution.py:21
  156.5 1.4 bitcast_dynamic-update-slice_fusion.3
  158.5 1.4 bitcast_dynamic-update-slice_fusion.3
  159.9 19.7 %custom-call.23 = f32[1,2,128,128]{2,3,1,0:T(8,128)S(1)} custom-call(f32[1,2,128,128]{3,2,1,0:T(8,128)S(1)} %bitcast.121), custom_call_target="InvertDiagBlocksLowerTriangular" | custom-call | tf_op jit(solution)/shard_map/vmap(jit(_cho_solve))/triangular_solve | solution.py:21
  181.3 35.7 %all_gather.6 = bf16[16,16,256]{2,1,0:T(8,128)(2,1)S(1)} all-gather(bf16[1,16,256]{2,1,0:T(8,128)(2,1)S(1)} %get-tuple-element.21), channel_id=1, replica_groups=mesh['leaf'=2,'rows'=16] {'rows'}, dimensions={0}, use_global_device_ids=true | all-gather | bytes 139264 | tf_op jit(solution)/shard_map/all_gather | solution.py:53
  217.4 29.8 %all-reduce.1 = f32[256]{0:T(256)S(1)} all-reduce(f32[256]{0:T(256)S(1)} %dynamic-update-slice.11), channel_id=2, replica_groups=mesh['leaf'=2,'rows'=16] {'rows'}, use_global_device_ids=true, to_apply=%add.1 | all-reduce | flops 256 | bytes 2048
  247.2 3.4 %fusion.3 = f32[16,16,512]{2,0,1:T(8,128)S(1)} fusion(bf16[16,512,256]{2,1,0:T(8,128)(2,1)} %gather_fusion, pred[16]{0:T(512)(128)(4,1)S(1)} %get-tuple-element.35, f32[16,16]{0,1:T(8,128)S(1)} %bitcast.120, pred[16,512]{1,0:T(8,128)(4,1)S(1)} %get-tuple-element.24, bf16[16,16,256]{2,1,0:T(8,128)(2,1)S(1)} %all_gather.6), kind=kOutput, calls=%fused_computation.12 | convolution fusion | flops 69468160 | bytes 4858896 | tf_op jit(solution)/shard_map/ncf,nsf->cns/dot_general | solution.py:57
  251.4 0.8 broadcast_select_fusion.9
  (53 shorter events, 11.9 us)
Async XLA Ops:
  7.2 17.6 %all-to-all-start.1 = ((bf16[16,2,256]{2,1,0:T(2,128)(2,1)}), bf16[16,2,256]{2,1,0:T(2,128)(2,1)S(1)}, u32[]{:S(2)}, u32[]{:S(2)}) async-start(bf16[16,2,256]{2,1,0:T(2,128)(2,1)} %reshape.402), calls=%async_computation.1 | async-start | bytes 32768 | tf_op jit(solution)/shard_map/all_to_all | solution.py:44
  24.8 6.3 %copy-start = (u32[32]{0:T(128)S(1)}, u32[32]{0:T(128)}, u32[]{:S(2)}) copy-start(u32[32]{0:T(128)} %constant.166) | copy-start | bytes 388
  24.8 83.7 %all-to-all-start = ((bf16[16,512,256]{2,1,0:T(8,128)(2,1)}), bf16[16,512,256]{2,1,0:T(8,128)(2,1)}, u32[]{:S(2)}, u32[]{:S(2)}) async-start(bf16[16,512,256]{2,1,0:T(8,128)(2,1)} %broadcast_select_fusion.1), calls=%async_computation | async-start | bytes 8388608 | tf_op jit(solution)/shard_map/all_to_all | solution.py:43
where the time goes:
time: 253 us; the launch traced here: 252 us
  waiting for transfers between devices  75.3 us (30%)
  other arithmetic  65.5 us (26%)
  blocking collectives  65.5 us (26%)
  local copies, waits for them, and re-layouts  15.1 us (6%)
  matrix products  14.3 us (6%)
  starting transfers between devices  13.6 us (5%)
  between operations  2.8 us (1%)
    all_to_all x1, waiting for transfers between devices, on_device(): lax.all_to_all(masked, 'rows', split_axis=0, concat_axis=1, tiled=True)  75.3 us
    all_gather x1, blocking collectives, on_device(): lax.all_gather(planes, 'rows', axis=0, tiled=True)  35.7 us
    another operation x7, other arithmetic, solve_nodes(): factor = jnp.linalg.cholesky(system)  34.8 us
    unnamed x1, blocking collectives  29.8 us
    another operation x3, other arithmetic, solve_nodes(): jax.scipy.linalg.cho_solve((lower, True), right.T)  19.7 us
    all_to_all x1, starting transfers between devices, on_device(): lax.all_to_all(tagged, 'rows', split_axis=0, concat_axis=1, tiled=True)  7.41 us
    all_to_all x1, starting transfers between devices, on_device(): lax.all_to_all(masked, 'rows', split_axis=0, concat_axis=1, tiled=True)  6.19 us
    select_n x1, other arithmetic, on_device(): jnp.where(live_rows[:, :, None], blocks, jnp.zeros((), jnp.bfloat16))  5.27 us
  transfers between devices with their start and end apart: 2, of which 1 were waited for; matrix products, arithmetic and copies ran while one was open for 5% of the time, Pallas kernels for 0%

commit v1 on v0

v1 whole, which is shorter than its diff:
```python
import functools
import jax
import jax.numpy as jnp
from jax import lax
from jax.experimental import pallas as pl
from jax.experimental.pallas import tpu as pltpu
from jax.sharding import PartitionSpec as P

CLASSES = 16
LANES = 128
RIDGE = 0.1
HIGHEST = lax.Precision.HIGHEST
TN = (((0,), (0,)), ((), ()))
NT = (((1,), (1,)), ((), ()))


def iota(shape, dim):
    return lax.broadcasted_iota(jnp.int32, shape, dim)


def partial_kernel(nodes_ref, x_ref, ids_ref, labels_ref, out_ref):
    step = pl.program_id(0)
    node = nodes_ref[step]
    seg, feat = x_ref.shape
    half = feat // 2
    pieces = seg // LANES
    ids = ids_ref[pl.ds(node * pieces, pieces), :]
    tags = labels_ref[pl.ds(node * pieces, pieces), :]
    live = ids == node
    length = jnp.sum(live.astype(jnp.int32))
    x = x_ref[...]
    x = jnp.where(iota((seg, feat), 0) < length, x, jnp.zeros((), x.dtype))
    tags = jnp.where(live, tags, -1)
    hot = jnp.concatenate(
        [tags[q : q + 1, :] == iota((CLASSES, LANES), 0) for q in range(pieces)], axis=1
    )
    hot = hot.astype(jnp.float32).astype(jnp.bfloat16)
    moment = lax.dot_general(x, x, TN, preferred_element_type=jnp.float32)
    sums = jnp.dot(hot, x, preferred_element_type=jnp.float32)
    counts = lax.dot_general(
        jnp.ones((8, seg), jnp.bfloat16), hot, NT, preferred_element_type=jnp.float32
    )
    row, col = iota((half, half), 0), iota((half, half), 1)
    low = moment[half:, half:]
    packed = jnp.where(row >= col, moment[:half, :half], low)
    diag = jnp.sum(jnp.where(row == col, low, 0.0), axis=0, keepdims=True)
    out_ref[0, 0:half, 0:half] = packed
    out_ref[0, 0:half, half:feat] = moment[:half, half:]
    out_ref[0, half : half + CLASSES, :] = sums
    top = half + CLASSES
    out_ref[0, top : top + 8, 0:half] = jnp.concatenate(
        [counts, jnp.zeros((8, half - CLASSES), jnp.float32)], axis=1
    )
    out_ref[0, top : top + 8, half:feat] = jnp.broadcast_to(diag, (8, half))


def partner_of(me, bit):
    width = 1 << bit
    return me + width * (1 - 2 * ((me // width) % 2))


def reduce_kernel(n, part_ref, out_ref, acc, landed, send_sems, recv_sems):
    bits = n.bit_length() - 1
    me = lax.axis_index("rows")
    barrier = pltpu.get_barrier_semaphore()
    for bit in range(bits):
        pl.semaphore_signal(barrier, inc=1, device_id={"rows": partner_of(me, bit)})
    pl.semaphore_wait(barrier, bits)

    def copy_of(step, q):
        half = n >> (step + 1)
        source = part_ref if step == 0 else acc
        return pltpu.make_async_remote_copy(
            src_ref=source.at[q],
            dst_ref=landed.at[q],
            send_sem=send_sems.at[q],
            recv_sem=recv_sems.at[q],
            device_id={"rows": partner_of(me, step)},
        )

    for q in reversed(range(n // 2, n)):
        copy_of(0, q).start()
    for step in range(bits):
        half = n >> (step + 1)
        for q in reversed(range(half)):
            copy_of(step, q + half).wait_recv()
            base = part_ref if step == 0 else acc
            total = base[q] + landed[q + half]
            if step == bits - 1:
                out_ref[...] = total
            else:
                acc[q] = total
                if q >= half // 2:
                    copy_of(step + 1, q).start()
    for step in range(bits):
        half = n >> (step + 1)
        for q in range(half, 2 * half):
            copy_of(step, q).wait_send()


def lane_of(x, lane):
    index = jnp.full(x.shape, lane, jnp.int32)
    return jnp.take_along_axis(x, index, axis=1, mode="promise_in_bounds")


def solve_kernel(sum_ref, planes_ref, message_ref, work):
    half = LANES
    feat = sum_ref.shape[1]
    top = half + CLASSES
    square = sum_ref[0:half, 0:half]
    turned = square.T
    row, col = iota((half, half), 0), iota((half, half), 1)
    diag = sum_ref[top : top + 1, half:feat]
    first = jnp.where(row >= col, square, turned)
    last = jnp.where(row < col, square, jnp.where(row == col, diag, turned))
    cross = sum_ref[0:half, half:feat]
    sums = sum_ref[half:top, :]
    count_row = sum_ref[top : top + 1, 0:CLASSES]
    eye = iota((CLASSES, CLASSES), 0) == iota((CLASSES, CLASSES), 1)
    counts = jnp.sum(jnp.where(eye, count_row, 0.0), axis=1, keepdims=True)
    total = jnp.sum(counts, axis=0, keepdims=True)
    centers = jnp.sum(sums, axis=0, keepdims=True) / total
    scaled = sums / jnp.maximum(counts, 1.0)
    between = lax.dot_general(
        scaled, sums, TN, precision=HIGHEST, preferred_element_type=jnp.float32
    )
    ridge = jnp.where(row == col, RIDGE, 0.0)
    work[0:half, 0:half] = (first - between[:half, :half]) / total + ridge
    work[0:half, half:feat] = (cross - between[:half, half:]) / total
    work[half:feat, 0:half] = (cross.T - between[half:, :half]) / total
    work[half:feat, half:feat] = (last - between[half:, half:]) / total + ridge
    work[feat : feat + CLASSES, :] = (sums - counts * centers) / total

    rows = feat + CLASSES
    lanes = iota((1, LANES), 1)

    def four(group, base, lane, tile, start):
        pivots = work[pl.ds(group, 8), tile * LANES : (tile + 1) * LANES]
        other = work[pl.ds(group, 8), (1 - tile) * LANES : (2 - tile) * LANES]
        spread = [lane_of(pivots, lane + u) for u in range(4)]
        d = [[spread[u][base + t : base + t + 1, :] for u in range(4)] for t in range(4)]
        a, b, c = d[0][0], d[0][1], d[1][1]
        inv = 1.0 / (a * c - b * b)
        p00, p01, p11 = c * inv, -b * inv, a * inv
        q00, q01, q10, q11 = d[0][2], d[0][3], d[1][2], d[1][3]
        t00, t01 = p00 * q00 + p01 * q10, p00 * q01 + p01 * q11
        t10, t11 = p01 * q00 + p11 * q10, p01 * q01 + p11 * q11
        s00 = d[2][2] - (q00 * t00 + q10 * t10)
        s01 = d[2][3] - (q00 * t01 + q10 * t11)
        s11 = d[3][3] - (q01 * t01 + q11 * t11)
        inv = 1.0 / (s00 * s11 - s01 * s01)
        h00, h01, h11 = s11 * inv, -s01 * inv, s00 * inv
        u00, u01 = t00 * h00 + t01 * h01, t00 * h01 + t01 * h11
        u10, u11 = t10 * h00 + t11 * h01, t10 * h01 + t11 * h11
        e00 = p00 + u00 * t00 + u01 * t01
        e01 = p01 + u00 * t10 + u01 * t11
        e11 = p11 + u10 * t10 + u11 * t11
        dinv = [
            [e00, e01, -u00, -u01],
            [e01, e11, -u10, -u11],
            [-u00, -u10, h00, h01],
            [-u01, -u11, h01, h11],
        ]
        inside = (lanes >= lane) & (lanes < lane + 4)
        near = [
            jnp.where(inside, jnp.where(lanes == lane + t, -1.0, 0.0), pivots[base + t : base + t + 1, :])
            for t in range(4)
        ]
        far = [other[base + t : base + t + 1, :] for t in range(4)]
        mix = lambda r, t: (dinv[t][0] * r[0] + dinv[t][1] * r[1]) + (dinv[t][2] * r[2] + dinv[t][3] * r[3])
        wn = [jnp.broadcast_to(mix(near, t), (8, LANES)) for t in range(4)]
        wf = [jnp.broadcast_to(mix(far, t), (8, LANES)) for t in range(4)]
        inside8 = jnp.broadcast_to(inside, (8, LANES))
        for g in range(start, rows, 8):
            x = work[g : g + 8, tile * LANES : (tile + 1) * LANES]
            y = work[g : g + 8, (1 - tile) * LANES : (2 - tile) * LANES]
            k = [lane_of(x, lane + u) for u in range(4)]
            x = jnp.where(inside8, 0.0, x)
            x = x - ((k[0] * wn[0] + k[1] * wn[1]) + (k[2] * wn[2] + k[3] * wn[3]))
            y = y - ((k[0] * wf[0] + k[1] * wf[1]) + (k[2] * wf[2] + k[3] * wf[3]))
            work[g : g + 8, tile * LANES : (tile + 1) * LANES] = x
            work[g : g + 8, (1 - tile) * LANES : (2 - tile) * LANES] = y

    span = 32
    for start in range(0, feat, span):
        tile = start // LANES

        def body(i, carry):
            group = pl.multiple_of(start + 8 * i, 8)
            lane = start % LANES + 8 * i
            four(group, 0, lane, tile, start)
            four(group, 4, lane + 4, tile, start)
            return carry

        lax.fori_loop(0, span // 8, body, 0)

    planes = work[feat : feat + CLASSES, :]
    planes_ref[...] = planes
    offsets = -jnp.sum(planes * centers, axis=1, keepdims=True)
    high = offsets.astype(jnp.bfloat16).astype(jnp.float32)
    middle = (offsets - high).astype(jnp.bfloat16).astype(jnp.float32)
    low = offsets - high - middle
    lane = iota((CLASSES, feat), 1)
    coded = jnp.where(lane < LANES, high, jnp.where(lane < LANES + LANES // 2, middle, low))
    message_ref[0:CLASSES, :] = planes.astype(jnp.bfloat16)
    message_ref[CLASSES : 2 * CLASSES, :] = coded.astype(jnp.bfloat16)


def gather_kernel(n, mine_ref, out_ref, local_sem, send_sems, recv_sems):
    me = lax.axis_index("rows")
    barrier = pltpu.get_barrier_semaphore()
    for shift in range(1, n):
        pl.semaphore_signal(barrier, inc=1, device_id={"rows": lax.rem(me + shift, n)})
    own = pltpu.make_async_copy(mine_ref, out_ref.at[me], local_sem)
    own.start()
    pl.semaphore_wait(barrier, n - 1)

    def copy_of(shift):
        return pltpu.make_async_remote_copy(
            src_ref=mine_ref,
            dst_ref=out_ref.at[me],
            send_sem=send_sems.at[shift],
            recv_sem=recv_sems.at[shift],
            device_id={"rows": lax.rem(me + shift, n)},
        )

    for shift in range(1, n):
        copy_of(shift).start()
    own.wait()
    for shift in range(1, n):
        copy_of(shift).wait()


def score_kernel(owners_ref, x_ref, ids_ref, message_ref, out_ref):
    node = pl.program_id(0)
    seg = x_ref.shape[0]
    pieces = seg // LANES
    planes = message_ref[0, 0:CLASSES, :]
    coded = message_ref[0, CLASSES : 2 * CLASSES, :].astype(jnp.float32)
    quarter = LANES + LANES // 2
    offsets = coded[:, 0:1] + coded[:, LANES : LANES + 1] + coded[:, quarter : quarter + 1]
    scores = lax.dot_general(planes, x_ref[...], NT, preferred_element_type=jnp.float32)
    scores = scores + offsets
    ids = ids_ref[pl.ds(node * pieces, pieces), :]
    for q in range(pieces):
        block = scores[:, q * LANES : (q + 1) * LANES]
        out_ref[:, q * LANES : (q + 1) * LANES] = jnp.where(ids[q : q + 1, :] == node, block, 0.0)


def reverse_bits(value, bits):
    return int(format(value, "0%db" % bits)[::-1], 2)


def on_device(features, node_ids, labels, owners):
    row_count, feat = features.shape
    n = owners.shape[0]
    seg = row_count // n
    bits = n.bit_length() - 1
    half = feat // 2
    depth = half + CLASSES + 8
    me = lax.axis_index("rows")
    ids = node_ids.reshape(row_count // LANES, LANES)
    tags = labels.reshape(row_count // LANES, LANES)
    order = iota((n, n), 0)
    flipped = sum(((order >> b) & 1) << (bits - 1 - b) for b in range(bits))
    slot = flipped ^ me
    nodes = jnp.sum(jnp.where(owners[None, :] == slot, iota((n, n), 1), 0), axis=1)

    whole = pl.BlockSpec(memory_space=pltpu.VMEM)
    parts = pl.pallas_call(
        partial_kernel,
        grid_spec=pltpu.PrefetchScalarGridSpec(
            num_scalar_prefetch=1,
            grid=(n,),
            in_specs=[pl.BlockSpec((seg, feat), lambda i, nodes: (nodes[i], 0)), whole, whole],
            out_specs=pl.BlockSpec((1, depth, feat), lambda i, nodes: (i, 0, 0)),
        ),
        out_shape=jax.ShapeDtypeStruct((n, depth, feat), jnp.float32),
        name="partials",
    )(nodes, features, ids, tags)

    summed = pl.pallas_call(
        functools.partial(reduce_kernel, n),
        out_shape=jax.ShapeDtypeStruct((depth, feat), jnp.float32),
        in_specs=[whole],
        out_specs=whole,
        scratch_shapes=[
            pltpu.VMEM((n // 2, depth, feat), jnp.float32),
            pltpu.VMEM((n, depth, feat), jnp.float32),
            pltpu.SemaphoreType.DMA((n,)),
            pltpu.SemaphoreType.DMA((n,)),
        ],
        compiler_params=pltpu.CompilerParams(
            collective_id=0, has_side_effects=True, vmem_limit_bytes=60 << 20
        ),
        name="halving",
    )(parts)

    planes, message = pl.pallas_call(
        solve_kernel,
        out_shape=(
            jax.ShapeDtypeStruct((CLASSES, feat), jnp.float32),
            jax.ShapeDtypeStruct((2 * CLASSES, feat), jnp.bfloat16),
        ),
        in_specs=[whole],
        out_specs=(whole, whole),
        scratch_shapes=[pltpu.VMEM((feat + CLASSES, feat), jnp.float32)],
        name="solve",
    )(summed)

    messages = pl.pallas_call(
        functools.partial(gather_kernel, n),
        out_shape=jax.ShapeDtypeStruct((n, 2 * CLASSES, feat), jnp.bfloat16),
        in_specs=[whole],
        out_specs=whole,
        scratch_shapes=[
            pltpu.SemaphoreType.DMA,
            pltpu.SemaphoreType.DMA((n,)),
            pltpu.SemaphoreType.DMA((n,)),
        ],
        compiler_params=pltpu.CompilerParams(collective_id=1, has_side_effects=True),
        name="spread",
    )(message)

    scores = pl.pallas_call(
        score_kernel,
        grid_spec=pltpu.PrefetchScalarGridSpec(
            num_scalar_prefetch=1,
            grid=(n,),
            in_specs=[
                pl.BlockSpec((seg, feat), lambda i, owners: (i, 0)),
                whole,
                pl.BlockSpec((1, 2 * CLASSES, feat), lambda i, owners: (owners[i], 0, 0)),
            ],
            out_specs=pl.BlockSpec((CLASSES, seg), lambda i, owners: (0, i)),
        ),
        out_shape=jax.ShapeDtypeStruct((CLASSES, row_count), jnp.float32),
        name="scores",
    )(owners, features, ids, messages)
    return planes[None], scores


def solution(mesh):
    in_specs = (P(("leaf", "rows"), None), P(("leaf", "rows")), P(("leaf", "rows")), P("leaf"))
    out_specs = (P(("leaf", "rows"), None, None), P(None, ("leaf", "rows")))
    return jax.shard_map(
        on_device, mesh=mesh, in_specs=in_specs, out_specs=out_specs, check_vma=False
    )
```

time: 253 us -> 91.8 us (0.36)
  Pallas kernels: 0 us -> 88.4 us
  waiting for transfers between devices: 75.3 us -> 0 us
  blocking collectives: 65.5 us -> 0 us
  other arithmetic: 65.5 us -> 1.36 us
  local copies, waits for them, and re-layouts: 15.1 us -> 0 us
  matrix products: 14.3 us -> 0 us
  starting transfers between devices: 13.6 us -> 0 us
    pallas_call x0 -> x5, Pallas kernels: none -> 88.4 us  [the longest x1 32.6 us: on_device(): pl.pallas_call(functools.partial(reduce_kernel, n), out_shape=jax.ShapeDt...]
    all_to_all x2 -> x0, waiting for transfers between devices: 75.3 us -> none  [the longest x1 75.3 us: on_device(): lax.all_to_all(masked, 'rows', split_axis=0, concat_axis=1, tiled=True)]
    another operation x10 -> x0, other arithmetic: 54.5 us -> none  [the longest x7 34.8 us: solve_nodes(): factor = jnp.linalg.cholesky(system)]
    all_gather x1 -> x0, blocking collectives: 35.7 us -> none  [on_device(): lax.all_gather(planes, 'rows', axis=0, tiled=True)]
    unnamed x1 -> x0, blocking collectives: 29.8 us -> none
    all_to_all x2 -> x0, starting transfers between devices: 13.6 us -> none  [the longest x1 7.41 us: on_device(): lax.all_to_all(tagged, 'rows', split_axis=0, concat_axis=1, tiled=True)]
    dot_general x5 -> x0, matrix products: 12.7 us -> none  [the longest x1 5.2 us: on_device(): jnp.einsum('nsf,nsg->nfg', arrived, arrived, preferred_element_type=jnp.f...]
    select_n x4 -> x0, other arithmetic: 6.78 us -> none  [the longest x1 5.27 us: on_device(): jnp.where(live_rows[:, :, None], blocks, jnp.zeros((), jnp.bfloat16))]
  transfers between devices with their start and end apart: 2 -> 0, of which waited for: 1 -> 0; matrix products, arithmetic and copies ran while one was open for 5% -> 0% of each run, Pallas kernels for 0% -> 0%
where the time goes in v1:
time: 91.8 us; the launch traced here: 90.4 us
  Pallas kernels  88.4 us (96%)
  other arithmetic  1.36 us (1%)
    pallas_call x1, Pallas kernels, on_device(): pl.pallas_call(functools.partial(reduce_kernel, n), out_shape=jax.ShapeDt...  32.6 us
    pallas_call x1, Pallas kernels, on_device(): pl.pallas_call(solve_kernel, out_shape=(jax.ShapeDtypeStruct((CLASSES, fe...  21.7 us
    pallas_call x1, Pallas kernels, on_device(): pl.pallas_call(partial_kernel, grid_spec=pltpu.PrefetchScalarGridSpec(num...  13.8 us
    pallas_call x1, Pallas kernels, on_device(): pl.pallas_call(score_kernel, grid_spec=pltpu.PrefetchScalarGridSpec(num_s...  11.3 us
    pallas_call x1, Pallas kernels, on_device(): pl.pallas_call(functools.partial(gather_kernel, n), out_shape=jax.ShapeDt...  9.07 us

profile of v1, /device:TPU:0, one launch (start us, length us, event | category | flops | bytes accessed | tf_op | source)
XLA Modules:
  0.0 90.4 jit_solution(8651933609007331454)
XLA Ops:
  0.6 1.4 %select_reduce_fusion.nodes_ref = s32[16]{0:T(128)} fusion(s32[16]{0:T(128)} %owners_ref.1, s32[16]{0:T(128)S(1)} %fusion.9), kind=kLoop, calls=%fused_computation | loop fusion | flops 752 | bytes 192 | tf_op jit(solution)/shard_map/reduce_sum | solution.py:267
  2.0 13.8 %partials.1.part_ref = f32[16,152,256]{2,1,0:T(8,128)} custom-call(s32[16]{0:T(128)} %select_reduce_fusion.nodes_ref, bf16[8192,256]{1,0:T(8,128)(2,1)} %x_ref.3, s32[64,128]{1,0:T(8,128)} %bitcast.3, s32[64,128]{1,0:T(8,128)} %bitcast.5), custom_call_target="tpu_custom_call" | custom-call | tf_op jit(solution)/shard_map/partials/pallas_call | solution.py:270
  15.8 32.6 %halving.1.sum_ref = f32[152,256]{1,0:T(8,128)} custom-call(f32[16,152,256]{2,1,0:T(8,128)} %partials.1.part_ref), custom_call_target="tpu_custom_call" | custom-call | tf_op jit(solution)/shard_map/halving/pallas_call | solution.py:282
  48.4 21.7 %solve.1 = (f32[16,256]{1,0:T(8,128)}, bf16[32,256]{1,0:T(8,128)(2,1)}) custom-call(f32[152,256]{1,0:T(8,128)} %halving.1.sum_ref), custom_call_target="tpu_custom_call" | custom-call | tf_op jit(solution)/shard_map/solve/pallas_call | solution.py:299
  70.0 9.1 %spread.1.message_ref = bf16[16,32,256]{2,1,0:T(8,128)(2,1)} custom-call(bf16[32,256]{1,0:T(8,128)(2,1)} %get-tuple-element.5.mine_ref), custom_call_target="tpu_custom_call" | custom-call | tf_op jit(solution)/shard_map/spread/pallas_call | solution.py:311
  79.1 11.3 %scores.1 = f32[16,8192]{1,0:T(8,128)} custom-call(s32[16]{0:T(128)} %owners_ref.1, bf16[8192,256]{1,0:T(8,128)(2,1)} %x_ref.3, s32[64,128]{1,0:T(8,128)} %bitcast.4, bf16[16,32,256]{2,1,0:T(8,128)(2,1)} %spread.1.message_ref), custom_call_target="tpu_custom_call" | custom-call | tf_op jit(solution)/shard_map/scores/pallas_call | solution.py:325
  (1 shorter events, 0.0 us)

commit v2 on v1

--- a/solution.py
+++ b/solution.py
@@ -18,21 +18,25 @@
     return lax.broadcasted_iota(jnp.int32, shape, dim)
 
 
-def partial_kernel(nodes_ref, x_ref, ids_ref, labels_ref, out_ref):
-    step = pl.program_id(0)
-    node = nodes_ref[step]
-    seg, feat = x_ref.shape
+def partner_of(me, bit):
+    width = 1 << bit
+    return me + width * (1 - 2 * ((me // width) % 2))
+
+
+def one_partial(node, q, x_ref, ids_ref, labels_ref, out_ref):
+    seg, feat = x_ref.shape[1:]
     half = feat // 2
     pieces = seg // LANES
     ids = ids_ref[pl.ds(node * pieces, pieces), :]
     tags = labels_ref[pl.ds(node * pieces, pieces), :]
     live = ids == node
-    length = jnp.sum(live.astype(jnp.int32))
-    x = x_ref[...]
-    x = jnp.where(iota((seg, feat), 0) < length, x, jnp.zeros((), x.dtype))
+    length = jnp.sum(live.astype(jnp.float32), axis=(0, 1), keepdims=True)
+    x = x_ref[node]
+    position = iota((seg, 1), 0).astype(jnp.float32)
+    x = jnp.where(position < length, x, jnp.zeros((), x.dtype))
     tags = jnp.where(live, tags, -1)
     hot = jnp.concatenate(
-        [tags[q : q + 1, :] == iota((CLASSES, LANES), 0) for q in range(pieces)], axis=1
+        [tags[k : k + 1, :] == iota((CLASSES, LANES), 0) for k in range(pieces)], axis=1
     )
     hot = hot.astype(jnp.float32).astype(jnp.bfloat16)
     moment = lax.dot_general(x, x, TN, preferred_element_type=jnp.float32)
@@ -44,48 +48,92 @@
     low = moment[half:, half:]
     packed = jnp.where(row >= col, moment[:half, :half], low)
     diag = jnp.sum(jnp.where(row == col, low, 0.0), axis=0, keepdims=True)
-    out_ref[0, 0:half, 0:half] = packed
-    out_ref[0, 0:half, half:feat] = moment[:half, half:]
-    out_ref[0, half : half + CLASSES, :] = sums
+    out_ref[q, 0:half, 0:half] = packed
+    out_ref[q, 0:half, half:feat] = moment[:half, half:]
+    out_ref[q, half : half + CLASSES, :] = sums
     top = half + CLASSES
-    out_ref[0, top : top + 8, 0:half] = jnp.concatenate(
+    out_ref[q, top : top + 8, 0:half] = jnp.concatenate(
         [counts, jnp.zeros((8, half - CLASSES), jnp.float32)], axis=1
     )
-    out_ref[0, top : top + 8, half:feat] = jnp.broadcast_to(diag, (8, half))
-
-
-def partner_of(me, bit):
-    width = 1 << bit
-    return me + width * (1 - 2 * ((me // width) % 2))
-
-
-def reduce_kernel(n, part_ref, out_ref, acc, landed, send_sems, recv_sems):
+    out_ref[q, top : top + 8, half:feat] = jnp.broadcast_to(diag, (8, half))
+
+
+def reduce_kernel(
+    n,
+    owners_hbm,
+    x_hbm,
+    ids_hbm,
+    labels_hbm,
+    out_ref,
+    owners_ref,
+    x_ref,
+    ids_ref,
+    labels_ref,
+    acc,
+    landed,
+    load_sems,
+    send_sems,
+    recv_sems,
+):
     bits = n.bit_length() - 1
     me = lax.axis_index("rows")
     barrier = pltpu.get_barrier_semaphore()
+    pairs = [(owners_hbm, owners_ref), (ids_hbm, ids_ref), (labels_hbm, labels_ref), (x_hbm, x_ref)]
+    loads = [pltpu.make_async_copy(a, b, load_sems.at[k]) for k, (a, b) in enumerate(pairs)]
+    for load in loads:
+        load.start()
     for bit in range(bits):
         pl.semaphore_signal(barrier, inc=1, device_id={"rows": partner_of(me, bit)})
+    for load in loads:
+        load.wait()
     pl.semaphore_wait(barrier, bits)
 
     def copy_of(step, q):
-        half = n >> (step + 1)
-        source = part_ref if step == 0 else acc
         return pltpu.make_async_remote_copy(
-            src_ref=source.at[q],
+            src_ref=acc.at[q],
             dst_ref=landed.at[q],
             send_sem=send_sems.at[q],
             recv_sem=recv_sems.at[q],
             device_id={"rows": partner_of(me, step)},
         )
 
-    for q in reversed(range(n // 2, n)):
-        copy_of(0, q).start()
-    for step in range(bits):
+    def partial(q):
+        slot = 0
+        for b in range(bits):
+            mine, theirs = (me // (1 << b)) % 2, (q // (1 << (bits - 1 - b))) % 2
+            slot = slot + (1 << b) * ((mine + theirs) % 2)
+        node = 0
+        for k in range(n):
+            node = jnp.where(owners_ref[k] == slot, k, node)
+        one_partial(node, q, x_ref, ids_ref, labels_ref, acc)
+
+    def finish(q):
+        copy_of(0, q + n // 2).wait_recv()
+        acc[q] = acc[q] + landed[q + n // 2]
+
+    def pair(i, carry):
+        q = n // 2 - 1 - i
+        partial(q + n // 2)
+        copy_of(0, q + n // 2).start()
+        partial(q)
+
+        @pl.when(i >= 1)
+        def _():
+            finish(q + 1)
+
+            @pl.when(q + 1 >= n // 4)
+            def _():
+                copy_of(1, q + 1).start()
+
+        return carry
+
+    lax.fori_loop(0, n // 2, pair, 0)
+    finish(0)
+    for step in range(1, bits):
         half = n >> (step + 1)
         for q in reversed(range(half)):
             copy_of(step, q + half).wait_recv()
-            base = part_ref if step == 0 else acc
-            total = base[q] + landed[q + half]
+            total = acc[q] + landed[q + half]
             if step == bits - 1:
                 out_ref[...] = total
             else:
@@ -99,8 +147,7 @@
 
 
 def lane_of(x, lane):
-    index = jnp.full(x.shape, lane, jnp.int32)
-    return jnp.take_along_axis(x, index, axis=1, mode="promise_in_bounds")
+    return jnp.broadcast_to(x[:, lane : lane + 1], x.shape)
 
 
 def solve_kernel(sum_ref, planes_ref, message_ref, work):
@@ -181,18 +228,9 @@
             work[g : g + 8, tile * LANES : (tile + 1) * LANES] = x
             work[g : g + 8, (1 - tile) * LANES : (2 - tile) * LANES] = y
 
-    span = 32
-    for start in range(0, feat, span):
-        tile = start // LANES
-
-        def body(i, carry):
-            group = pl.multiple_of(start + 8 * i, 8)
-            lane = start % LANES + 8 * i
-            four(group, 0, lane, tile, start)
-            four(group, 4, lane + 4, tile, start)
-            return carry
-
-        lax.fori_loop(0, span // 8, body, 0)
+    for pivot in range(0, feat, 4):
+        group, base = pivot // 8 * 8, pivot % 8
+        four(group, base, pivot % LANES, pivot // LANES, group if base == 0 else group + 8)
 
     planes = work[feat : feat + CLASSES, :]
     planes_ref[...] = planes
@@ -206,95 +244,102 @@
     message_ref[CLASSES : 2 * CLASSES, :] = coded.astype(jnp.bfloat16)
 
 
-def gather_kernel(n, mine_ref, out_ref, local_sem, send_sems, recv_sems):
+def gather_kernel(n, mine_ref, out_ref, local_sem, send_sems, recv_sems, on_sems, got_sems):
     me = lax.axis_index("rows")
+    near = partner_of(me, 0)
     barrier = pltpu.get_barrier_semaphore()
-    for shift in range(1, n):
-        pl.semaphore_signal(barrier, inc=1, device_id={"rows": lax.rem(me + shift, n)})
+    for t in range(1, n // 2):
+        pl.semaphore_signal(barrier, inc=1, device_id={"rows": lax.rem(me + 2 * t, n)})
+    pl.semaphore_signal(barrier, inc=1, device_id={"rows": near})
     own = pltpu.make_async_copy(mine_ref, out_ref.at[me], local_sem)
     own.start()
-    pl.semaphore_wait(barrier, n - 1)
-
-    def copy_of(shift):
+    pl.semaphore_wait(barrier, n // 2)
+
+    def far_copy(t):
         return pltpu.make_async_remote_copy(
             src_ref=mine_ref,
             dst_ref=out_ref.at[me],
-            send_sem=send_sems.at[shift],
-            recv_sem=recv_sems.at[shift],
-            device_id={"rows": lax.rem(me + shift, n)},
+            send_sem=send_sems.at[t],
+            recv_sem=recv_sems.at[t],
+            device_id={"rows": lax.rem(me + 2 * t, n)},
         )
 
-    for shift in range(1, n):
-        copy_of(shift).start()
+    def near_copy(t):
+        source = lax.rem(me + n - 2 * t, n)
+        return pltpu.make_async_remote_copy(
+            src_ref=mine_ref if t == 0 else out_ref.at[source],
+            dst_ref=out_ref.at[source],
+            send_sem=on_sems.at[t],
+            recv_sem=got_sems.at[t],
+            device_id={"rows": near},
+        )
+
+    turns = sorted(range(1, n // 2), key=lambda t: -min(t, n // 2 - t))
+    for t in turns:
+        far_copy(t).start()
+    near_copy(0).start()
     own.wait()
-    for shift in range(1, n):
-        copy_of(shift).wait()
-
-
-def score_kernel(owners_ref, x_ref, ids_ref, message_ref, out_ref):
-    node = pl.program_id(0)
-    seg = x_ref.shape[0]
+    for t in reversed(turns):
+        far_copy(t).wait_recv()
+        near_copy(t).start()
+    for t in turns:
+        far_copy(t).wait_send()
+    for t in range(n // 2):
+        near_copy(t).wait()
+
+
+def score_kernel(n, owners_ref, x_ref, ids_ref, message_ref, out_ref):
+    seg = x_ref.shape[0] * pl.num_programs(0) // n
+    some = x_ref.shape[0] // seg
     pieces = seg // LANES
-    planes = message_ref[0, 0:CLASSES, :]
-    coded = message_ref[0, CLASSES : 2 * CLASSES, :].astype(jnp.float32)
     quarter = LANES + LANES // 2
-    offsets = coded[:, 0:1] + coded[:, LANES : LANES + 1] + coded[:, quarter : quarter + 1]
-    scores = lax.dot_general(planes, x_ref[...], NT, preferred_element_type=jnp.float32)
-    scores = scores + offsets
-    ids = ids_ref[pl.ds(node * pieces, pieces), :]
-    for q in range(pieces):
-        block = scores[:, q * LANES : (q + 1) * LANES]
-        out_ref[:, q * LANES : (q + 1) * LANES] = jnp.where(ids[q : q + 1, :] == node, block, 0.0)
-
-
-def reverse_bits(value, bits):
-    return int(format(value, "0%db" % bits)[::-1], 2)
+    for k in range(some):
+        node = pl.program_id(0) * some + k
+        block = owners_ref[node]
+        planes = message_ref[block, 0:CLASSES, :]
+        coded = message_ref[block, CLASSES : 2 * CLASSES, :].astype(jnp.float32)
+        offsets = coded[:, 0:1] + coded[:, LANES : LANES + 1] + coded[:, quarter : quarter + 1]
+        rows = x_ref[k * seg : (k + 1) * seg, :]
+        scores = lax.dot_general(planes, rows, NT, preferred_element_type=jnp.float32)
+        scores = scores + offsets
+        ids = ids_ref[pl.ds(node * pieces, pieces), :]
+        for q in range(pieces):
+            part = scores[:, q * LANES : (q + 1) * LANES]
+            at = k * seg + q * LANES
+            out_ref[:, at : at + LANES] = jnp.where(ids[q : q + 1, :] == node, part, 0.0)
 
 
 def on_device(features, node_ids, labels, owners):
     row_count, feat = features.shape
     n = owners.shape[0]
     seg = row_count // n
-    bits = n.bit_length() - 1
     half = feat // 2
     depth = half + CLASSES + 8
-    me = lax.axis_index("rows")
     ids = node_ids.reshape(row_count // LANES, LANES)
     tags = labels.reshape(row_count // LANES, LANES)
-    order = iota((n, n), 0)
-    flipped = sum(((order >> b) & 1) << (bits - 1 - b) for b in range(bits))
-    slot = flipped ^ me
-    nodes = jnp.sum(jnp.where(owners[None, :] == slot, iota((n, n), 1), 0), axis=1)
 
     whole = pl.BlockSpec(memory_space=pltpu.VMEM)
-    parts = pl.pallas_call(
-        partial_kernel,
-        grid_spec=pltpu.PrefetchScalarGridSpec(
-            num_scalar_prefetch=1,
-            grid=(n,),
-            in_specs=[pl.BlockSpec((seg, feat), lambda i, nodes: (nodes[i], 0)), whole, whole],
-            out_specs=pl.BlockSpec((1, depth, feat), lambda i, nodes: (i, 0, 0)),
-        ),
-        out_shape=jax.ShapeDtypeStruct((n, depth, feat), jnp.float32),
-        name="partials",
-    )(nodes, features, ids, tags)
-
     summed = pl.pallas_call(
         functools.partial(reduce_kernel, n),
         out_shape=jax.ShapeDtypeStruct((depth, feat), jnp.float32),
-        in_specs=[whole],
+        in_specs=[pl.BlockSpec(memory_space=pltpu.HBM)] * 4,
         out_specs=whole,
         scratch_shapes=[
-            pltpu.VMEM((n // 2, depth, feat), jnp.float32),
+            pltpu.SMEM((n,), jnp.int32),
+            pltpu.VMEM((n, seg, feat), features.dtype),
+            pltpu.VMEM(ids.shape, jnp.int32),
+            pltpu.VMEM(ids.shape, jnp.int32),
             pltpu.VMEM((n, depth, feat), jnp.float32),
+            pltpu.VMEM((n, depth, feat), jnp.float32),
+            pltpu.SemaphoreType.DMA((4,)),
             pltpu.SemaphoreType.DMA((n,)),
             pltpu.SemaphoreType.DMA((n,)),
         ],
         compiler_params=pltpu.CompilerParams(
-            collective_id=0, has_side_effects=True, vmem_limit_bytes=60 << 20
+            collective_id=0, has_side_effects=True, vmem_limit_bytes=63 << 20
         ),
         name="halving",
-    )(parts)
+    )(owners, features.reshape(n, seg, feat), ids, tags)
 
     planes, message = pl.pallas_call(
         solve_kernel,
@@ -315,24 +360,27 @@
         out_specs=whole,
         scratch_shapes=[
             pltpu.SemaphoreType.DMA,
-            pltpu.SemaphoreType.DMA((n,)),
-            pltpu.SemaphoreType.DMA((n,)),
+            pltpu.SemaphoreType.DMA((n // 2,)),
+            pltpu.SemaphoreType.DMA((n // 2,)),
+            pltpu.SemaphoreType.DMA((n // 2,)),
+            pltpu.SemaphoreType.DMA((n // 2,)),
         ],
         compiler_params=pltpu.CompilerParams(collective_id=1, has_side_effects=True),
         name="spread",
     )(message)
 
+    some = 4
     scores = pl.pallas_call(
-        score_kernel,
+        functools.partial(score_kernel, n),
         grid_spec=pltpu.PrefetchScalarGridSpec(
             num_scalar_prefetch=1,
-            grid=(n,),
+            grid=(n // some,),
             in_specs=[
-                pl.BlockSpec((seg, feat), lambda i, owners: (i, 0)),
+                pl.BlockSpec((some * seg, feat), lambda i, owners: (i, 0)),
                 whole,
-                pl.BlockSpec((1, 2 * CLASSES, feat), lambda i, owners: (owners[i], 0, 0)),
+                whole,
             ],
-            out_specs=pl.BlockSpec((CLASSES, seg), lambda i, owners: (0, i)),
+            out_specs=pl.BlockSpec((CLASSES, some * seg), lambda i, owners: (0, i)),
         ),
         out_shape=jax.ShapeDtypeStruct((CLASSES, row_count), jnp.float32),
         name="scores",

time: 91.8 us -> 61.2 us (0.67); the launches traced: 90.4 us -> 60.9 us
  Pallas kernels: 88.4 us -> 60.2 us
  other arithmetic: 1.36 us -> 0 us
    pallas_call x2 -> x1, Pallas kernels: 25.1 us -> 5.35 us  [on_device(): pl.pallas_call(functools.partial(score_kernel, n), grid_spec=pltpu.Prefet...]
    pallas_call x1, Pallas kernels: 21.7 us -> 13 us  [on_device(): pl.pallas_call(solve_kernel, out_shape=(jax.ShapeDtypeStruct((CLASSES, fe...]
    reduce_sum x1 -> x0, other arithmetic: 1.35 us -> none  [on_device(): jnp.sum(jnp.where(owners[None, :] == slot, iota((n, n), 1), 0), axis=1)]
where the time goes in v2:
time: 61.2 us; the launch traced here: 60.9 us
  Pallas kernels  60.2 us (98%)
  between operations  0.65 us (1%)
    pallas_call x1, Pallas kernels, on_device(): pl.pallas_call(functools.partial(reduce_kernel, n), out_shape=jax.ShapeDt...  31.9 us
    pallas_call x1, Pallas kernels, on_device(): pl.pallas_call(solve_kernel, out_shape=(jax.ShapeDtypeStruct((CLASSES, fe...  13 us
    pallas_call x1, Pallas kernels, on_device(): pl.pallas_call(functools.partial(gather_kernel, n), out_shape=jax.ShapeDt...  9.97 us
    pallas_call x1, Pallas kernels, on_device(): pl.pallas_call(functools.partial(score_kernel, n), grid_spec=pltpu.Prefet...  5.35 us

profile of v2, /device:TPU:0, one launch (start us, length us, event | category | flops | bytes accessed | tf_op | source)
XLA Modules:
  0.0 60.9 jit_solution(17159636889174563309)
XLA Ops:
  0.6 31.9 %halving.1.sum_ref = f32[152,256]{1,0:T(8,128)} custom-call(s32[16]{0:T(128)} %owners_ref.1, bf16[16,512,256]{2,1,0:T(8,128)(2,1)} %bitcast.4, s32[64,128]{1,0:T(8,128)} %bitcast.5, s32[64,128]{1,0:T(8,128)} %bitcast.7), custom_call_target="tpu_custom_call" | custom-call | tf_op jit(solution)/shard_map/halving/pallas_call | solution.py:322
  32.5 13.0 %solve.1 = (f32[16,256]{1,0:T(8,128)}, bf16[32,256]{1,0:T(8,128)(2,1)}) custom-call(f32[152,256]{1,0:T(8,128)} %halving.1.sum_ref), custom_call_target="tpu_custom_call" | custom-call | tf_op jit(solution)/shard_map/solve/pallas_call | solution.py:344
  45.6 10.0 %spread.1.message_ref = bf16[16,32,256]{2,1,0:T(8,128)(2,1)} custom-call(bf16[32,256]{1,0:T(8,128)(2,1)} %get-tuple-element.5.mine_ref), custom_call_target="tpu_custom_call" | custom-call | tf_op jit(solution)/shard_map/spread/pallas_call | solution.py:356
  55.5 5.3 %scores.1 = f32[16,8192]{1,0:T(8,128)} custom-call(s32[16]{0:T(128)} %owners_ref.1, bf16[8192,256]{1,0:T(8,128)(2,1)} %x_ref.1, s32[64,128]{1,0:T(8,128)} %bitcast.6, bf16[16,32,256]{2,1,0:T(8,128)(2,1)} %spread.1.message_ref), custom_call_target="tpu_custom_call" | custom-call | tf_op jit(solution)/shard_map/scores/pallas_call | solution.py:373

commit v3 on v2

--- a/solution.py
+++ b/solution.py
@@ -107,39 +107,65 @@
             node = jnp.where(owners_ref[k] == slot, k, node)
         one_partial(node, q, x_ref, ids_ref, labels_ref, acc)
 
-    def finish(q):
-        copy_of(0, q + n // 2).wait_recv()
-        acc[q] = acc[q] + landed[q + n // 2]
+    def finish(step, q):
+        half = n >> (step + 1)
+        copy_of(step, q + half).wait_recv()
+        acc[q] = acc[q] + landed[q + half]
+
+    quarter = n // 4
+
+    def turn(i):
+        low = quarter - 1 - i % quarter
+        for b in range(bits - 2):
+            yield (low // (1 << b)) % 2, bits - 3 - b
+        yield 1 - i // quarter, bits - 2
+
+    def block_at(i):
+        return sum(bit * (1 << place) for bit, place in turn(i))
 
     def pair(i, carry):
-        q = n // 2 - 1 - i
+        q = block_at(i)
         partial(q + n // 2)
         copy_of(0, q + n // 2).start()
         partial(q)
 
         @pl.when(i >= 1)
         def _():
-            finish(q + 1)
-
-            @pl.when(q + 1 >= n // 4)
+            before = block_at(i - 1)
+            finish(0, before)
+
+            @pl.when(i - 1 < quarter)
             def _():
-                copy_of(1, q + 1).start()
+                copy_of(1, before).start()
+
+        @pl.when(i >= quarter + 2)
+        def _():
+            before = block_at(i - 2)
+            finish(1, before)
+
+            @pl.when(before >= n // 8)
+            def _():
+                copy_of(2, before).start()
 
         return carry
 
     lax.fori_loop(0, n // 2, pair, 0)
-    finish(0)
+    finish(0, 0)
+    ready = {(0, block_at(i)): i for i in range(n // 2)}
     for step in range(1, bits):
         half = n >> (step + 1)
-        for q in reversed(range(half)):
-            copy_of(step, q + half).wait_recv()
-            total = acc[q] + landed[q + half]
-            if step == bits - 1:
-                out_ref[...] = total
-            else:
-                acc[q] = total
-                if q >= half // 2:
-                    copy_of(step + 1, q).start()
+        for q in range(half):
+            ready[step, q] = max(ready[step - 1, q], ready[step - 1, q + half] + 1)
+    late = {block_at(n // 2 - 2), block_at(n // 2 - 1)}
+    rest = [(step, q) for step, q in ready if step > 1 or (step == 1 and q in late)]
+    for step, q in sorted(rest, key=lambda event: (ready[event], event)):
+        if step == bits - 1:
+            copy_of(step, 1).wait_recv()
+            out_ref[...] = acc[0] + landed[1]
+        else:
+            finish(step, q)
+            if q >= n >> (step + 2):
+                copy_of(step + 1, q).start()
     for step in range(bits):
         half = n >> (step + 1)
         for q in range(half, 2 * half):

time: 61.2 us -> 56.7 us (0.926)
  Pallas kernels: 60.2 us -> 55.8 us
    pallas_call x1, Pallas kernels: 31.9 us -> 27.4 us  [on_device(): pl.pallas_call(functools.partial(reduce_kernel, n), out_shape=jax.ShapeDt...]
where the time goes in v3:
time: 56.7 us; the launch traced here: 56.4 us
  Pallas kernels  55.8 us (98%)
  between operations  0.65 us (1%)
    pallas_call x1, Pallas kernels, on_device(): pl.pallas_call(functools.partial(reduce_kernel, n), out_shape=jax.ShapeDt...  27.4 us
    pallas_call x1, Pallas kernels, on_device(): pl.pallas_call(solve_kernel, out_shape=(jax.ShapeDtypeStruct((CLASSES, fe...  13 us
    pallas_call x1, Pallas kernels, on_device(): pl.pallas_call(functools.partial(gather_kernel, n), out_shape=jax.ShapeDt...  9.97 us
    pallas_call x1, Pallas kernels, on_device(): pl.pallas_call(functools.partial(score_kernel, n), grid_spec=pltpu.Prefet...  5.35 us

profile of v3, /device:TPU:0, one launch (start us, length us, event | category | flops | bytes accessed | tf_op | source)
XLA Modules:
  0.0 56.4 jit_solution(1846852057167135309)
XLA Ops:
  0.6 27.4 %halving.1.sum_ref = f32[152,256]{1,0:T(8,128)} custom-call(s32[16]{0:T(128)} %owners_ref.1, bf16[16,512,256]{2,1,0:T(8,128)(2,1)} %bitcast.4, s32[64,128]{1,0:T(8,128)} %bitcast.5, s32[64,128]{1,0:T(8,128)} %bitcast.7), custom_call_target="tpu_custom_call" | custom-call | tf_op jit(solution)/shard_map/halving/pallas_call | solution.py:348
  28.0 13.0 %solve.1 = (f32[16,256]{1,0:T(8,128)}, bf16[32,256]{1,0:T(8,128)(2,1)}) custom-call(f32[152,256]{1,0:T(8,128)} %halving.1.sum_ref), custom_call_target="tpu_custom_call" | custom-call | tf_op jit(solution)/shard_map/solve/pallas_call | solution.py:370
  41.1 10.0 %spread.1.message_ref = bf16[16,32,256]{2,1,0:T(8,128)(2,1)} custom-call(bf16[32,256]{1,0:T(8,128)(2,1)} %get-tuple-element.5.mine_ref), custom_call_target="tpu_custom_call" | custom-call | tf_op jit(solution)/shard_map/spread/pallas_call | solution.py:382
  51.1 5.3 %scores.1 = f32[16,8192]{1,0:T(8,128)} custom-call(s32[16]{0:T(128)} %owners_ref.1, bf16[8192,256]{1,0:T(8,128)(2,1)} %x_ref.1, s32[64,128]{1,0:T(8,128)} %bitcast.6, bf16[16,32,256]{2,1,0:T(8,128)(2,1)} %spread.1.message_ref), custom_call_target="tpu_custom_call" | custom-call | tf_op jit(solution)/shard_map/scores/pallas_call | solution.py:399
